TPU v7x, 256 devices: a whole 4x4x8 slice. The times are simulated.
256 devices in a mesh: row: 16 (over z, core), col: 16 (over x, y).
Axes of the slice: x: 4, y: 4, z: 8, core: 2. Of those that a mesh axis runs over, the one named last changes fastest.
Arguments:
- matrix: bfloat16 [7, 4096, 7, 4096], P(None, 'row', None, 'col'), may hold values from -1 to 3
- pivots: int32 [2, 256], replicated, may hold values from 256 to 28671, as said below
Outputs:
- factored: bfloat16 [7, 4096, 7, 4096], P(None, 'row', None, 'col')
Inputs may be any that keep to these rules, and one draw needn't show every extreme that they name: Within a step s the pivots[s, :] are distinct and lie in (s + 1) * 256 to 28671.
All inputs are finite; a program needn't handle non-finite values.
Results may differ from a plain program's by a relative error of at most 0.0059.
Values may be sent and summed in bfloat16 or wider, within the bound.
A program may use at most 64 MiB of HBM per device.

v0:
```python
import jax
import jax.numpy as jnp
from jax import lax
from jax.sharding import PartitionSpec as P

STEPS = 2
NEWTON = 3


def broadcast(shard, axis, root):
    mine = lax.axis_index(axis) == root
    return lax.psum(jnp.where(mine, shard, jnp.zeros_like(shard)), axis)


def newton_inverse(diag_block):
    identity = jnp.eye(diag_block.shape[0], dtype=jnp.float32)
    approx = identity / 3.0
    for _ in range(NEWTON):
        product = jnp.dot(diag_block, approx, precision=lax.Precision.HIGHEST)
        approx = jnp.dot(approx, 2.0 * identity - product, precision=lax.Precision.HIGHEST)
    return approx


def body(matrix, pivots):
    row_count = lax.axis_size("row")
    col_count = lax.axis_size("col")
    row_index = lax.axis_index("row")
    col_index = lax.axis_index("col")
    row_cycles, block_size, col_cycles, _ = matrix.shape
    local_rows = row_cycles * block_size
    local_cols = col_cycles * block_size
    current = matrix.reshape(local_rows, local_cols)
    row_positions = jnp.arange(local_rows, dtype=jnp.int32)
    col_positions = jnp.arange(local_cols, dtype=jnp.int32)
    global_row = (
        row_positions // block_size * row_count * block_size
        + row_index * block_size
        + row_positions % block_size
    )
    global_col = (
        col_positions // block_size * col_count * block_size
        + col_index * block_size
        + col_positions % block_size
    )
    identity = jnp.eye(block_size, dtype=jnp.float32)
    for panel_step in range(STEPS):
        after_row = (panel_step + 1) * block_size
        owner_row = panel_step % row_count
        owner_cycle = panel_step // row_count
        owner_col = panel_step % col_count
        panel_cycle = panel_step // col_count
        chosen = pivots[panel_step]
        owner_of = chosen // block_size % row_count
        local_at = chosen // (block_size * row_count) * block_size + chosen % block_size
        is_mine = owner_of == row_index
        picked = jnp.where(
            is_mine[:, None],
            current[jnp.clip(local_at, 0, local_rows - 1)],
            jnp.zeros((), jnp.bfloat16),
        )
        top_rows = current[owner_cycle * block_size : (owner_cycle + 1) * block_size]
        is_top = row_index == owner_row
        new_top = lax.psum(picked, "row").astype(jnp.float32).astype(jnp.bfloat16)
        old_top = broadcast(top_rows, "row", owner_row)
        target = jnp.where(is_mine, local_at, local_rows)
        current = current.at[target].set(old_top, mode="drop")
        kept_rows = current[owner_cycle * block_size : (owner_cycle + 1) * block_size]
        current = current.at[owner_cycle * block_size : (owner_cycle + 1) * block_size].set(
            jnp.where(is_top, new_top, kept_rows)
        )
        panel_block = current[:, panel_cycle * block_size : (panel_cycle + 1) * block_size]
        is_owner = col_index == owner_col
        diag_block = jnp.where(
            is_owner,
            new_top[:, panel_cycle * block_size : (panel_cycle + 1) * block_size].astype(
                jnp.float32
            ),
            3.0 * identity,
        )
        below_mask = (global_row >= after_row)[:, None]
        inverse = newton_inverse(diag_block)
        own_lower = jnp.where(
            below_mask,
            jnp.dot(panel_block.astype(jnp.float32), inverse, precision=lax.Precision.HIGHEST),
            0.0,
        ).astype(jnp.bfloat16)
        lower_panel = broadcast(own_lower, "col", owner_col)
        right_mask = (global_col >= after_row)[None, :]
        upper_rows = jnp.where(right_mask, new_top, jnp.zeros_like(new_top))
        change = jnp.dot(lower_panel, upper_rows, preferred_element_type=jnp.float32)
        current = (current.astype(jnp.float32) - change).astype(jnp.bfloat16)
        old_panel = current[:, panel_cycle * block_size : (panel_cycle + 1) * block_size]
        current = current.at[:, panel_cycle * block_size : (panel_cycle + 1) * block_size].set(
            jnp.where(jnp.logical_and(is_owner, below_mask), lower_panel, old_panel)
        )
    return current.reshape(row_cycles, block_size, col_cycles, block_size)


def solution(mesh):
    return jax.shard_map(
        body,
        mesh=mesh,
        in_specs=(P(None, "row", None, "col"), P()),
        out_specs=P(None, "row", None, "col"),
        check_vma=False,
    )
```

profile of v0, /device:TPU:3, one launch (start us, length us, event | category | flops | bytes accessed | tf_op | source)
XLA Modules:
  0.0 544.1 jit_solution(16321497234872604605)
XLA Ops:
  6.5 0.0 all-reduce.13.cloned.1.call-start
  6.5 0.0 copy-start.4
  6.5 6.8 %copy.6 = bf16[7,256,7,256]{3,2,1,0:T(8,128)(2,1)S(1)} copy(bf16[7,256,7,256]{3,1,2,0:T(8,128)(2,1)} %param.10) | data formatting | bytes 12845056 | tf_op args[0]
  13.4 0.0 copy-done.4
  13.4 0.0 slice-start
  13.4 5.6 %copy.11 = bf16[224,8,7,256]{3,1,2,0:T(8,128)(2,1)} copy(bf16[224,8,7,256]{3,2,1,0:T(8,128)(2,1)S(1)} %bitcast.68) | data formatting | bytes 12845056
  19.0 0.0 slice-done
  19.0 0.6 copy.10
  19.7 0.1 broadcast_select_fusion.2
  19.7 1.4 copy.8
  21.2 5.8 %gather_fusion = bf16[256,1792]{1,0:T(8,128)(2,1)S(1)} fusion(bf16[1792,1792]{1,0:T(8,128)(2,1)} %bitcast.66, s32[1024]{0:T(1024)S(1)} %pad_clamp_fusion.1), kind=kCustom, calls=%fused_computation | custom fusion | bytes 1836032 | tf_op jit(solution)/shard_map/gather | solution.py:58
  27.0 1.1 broadcast_select_fusion.1
  28.0 0.0 all-reduce.13.cloned.1.call-update
  28.1 0.5 all-reduce.7.cloned.1.call-start
  28.6 117.3 %all-reduce.13.cloned.1.call-done = (bf16[256,1792]{1,0:T(8,128)(2,1)}, bf16[256,1792]{1,0:T(8,128)(2,1)}) async-done(((bf16[256,1792]{1,0:T(8,128)(2,1)}, bf16[256,1792]{1,0:T(8,128)(2,1)}), (bf16[256,1792]{1,0:T(8,128)(2,1)}, bf16[256,1792]{1,0:T(8,128)(2,1)})) %all-reduce.13.cloned.1.call-update) | async-done | bytes 1835024 | tf_op jit(solution)/shard_map/psum | solution.py:12
  145.9 0.0 copy-start.2
  145.9 9.5 %scatter_fusion = bf16[1792,1792]{1,0:T(8,128)(2,1)} fusion(bf16[1792,1792]{1,0:T(8,128)(2,1)} %bitcast.67, s32[256]{0:T(256)S(1)} %bitcast.70, bf16[256,1792]{1,0:T(8,128)(2,1)} %get-tuple-element.55), kind=kCustom, calls=%fused_computation.2 | custom fusion | bytes 2753536 | tf_op jit(solution)/shard_map/scatter | solution.py:66
  155.4 0.0 copy-done.2
  155.4 2.3 fusion.9
  157.7 0.4 convolution_subtract_fusion.5
  158.1 0.4 fusion.17
  158.5 0.4 convolution_subtract_fusion.4
  158.9 0.4 fusion.99
  159.3 0.4 convolution_subtract_fusion.3
  159.7 0.4 fusion.100
  160.1 3.1 fusion.3
  163.1 0.0 all-reduce.7.cloned.1.call-update
  163.2 0.2 all-reduce.11.cloned.1.call-start
  163.4 0.6 compare_reduce_fusion
  164.1 93.6 %all-reduce.7.cloned.1.call-done = bf16[1792,256]{1,0:T(8,128)(2,1)} async-done(((bf16[1792,256]{1,0:T(8,128)(2,1)}), bf16[1792,256]{1,0:T(8,128)(2,1)}) %all-reduce.7.cloned.1.call-update) | async-done | bytes 917520 | tf_op jit(solution)/shard_map/psum | solution.py:12
  257.7 0.0 copy-start
  257.7 7.8 %subtract_convert_fusion.1 = bf16[1792,1792]{1,0:T(8,128)(2,1)} fusion(bf16[1792,1792]{1,0:T(8,128)(2,1)} %fusion.9, bf16[1792,256]{1,0:T(8,128)(2,1)} %all-reduce.7.cloned.1.call-done, bf16[256,1792]{1,0:T(8,128)(2,1)S(1)} %copy-done.2, pred[1792]{0:T(1024)(128)(4,1)S(1)} %fusion.67), kind=kOutput, calls=%fused_computation.5 | convolution fusion | flops 1654259712 | bytes 14681856 | tf_op jit(solution)/shard_map/dot_general | solution.py:90
  265.5 0.0 copy-done
  265.5 3.3 fusion.4
  268.8 5.8 %gather_fusion.1 = bf16[256,1792]{1,0:T(8,128)(2,1)S(1)} fusion(bf16[1792,1792]{1,0:T(8,128)(2,1)} %fusion.4, s32[1024]{0:T(1024)S(1)} %pad_clamp_fusion), kind=kCustom, calls=%fused_computation.1 | custom fusion | bytes 1836032 | tf_op jit(solution)/shard_map/gather | solution.py:58
  274.6 2.6 slice_select_fusion.1
  277.2 0.0 all-reduce.11.cloned.1.call-update
  277.2 0.0 all-reduce.9.cloned.1.call-start
  277.3 116.4 %all-reduce.11.cloned.1.call-done = (bf16[256,1792]{1,0:T(8,128)(2,1)}, bf16[256,1792]{1,0:T(8,128)(2,1)}) async-done(((bf16[256,1792]{1,0:T(8,128)(2,1)}, bf16[256,1792]{1,0:T(8,128)(2,1)}), (bf16[256,1792]{1,0:T(8,128)(2,1)}, bf16[256,1792]{1,0:T(8,128)(2,1)})) %all-reduce.11.cloned.1.call-update) | async-done | bytes 1835024 | tf_op jit(solution)/shard_map/psum | solution.py:12
  393.7 0.0 copy-start.3
  393.7 9.7 %scatter_fusion.1 = bf16[1792,1792]{1,0:T(8,128)(2,1)} fusion(bf16[1792,1792]{1,0:T(8,128)(2,1)} %fusion.4, s32[256]{0:T(256)S(1)} %bitcast.71, bf16[256,1792]{1,0:T(8,128)(2,1)} %get-tuple-element.53), kind=kCustom, calls=%fused_computation.3 | custom fusion | bytes 2753536 | tf_op jit(solution)/shard_map/scatter | solution.py:66
  403.4 0.0 copy-done.3
  403.4 2.3 fusion.7
  405.7 0.4 convolution_subtract_fusion.2
  406.1 0.4 fusion.14
  406.5 0.4 convolution_subtract_fusion.1
  406.9 0.4 fusion.101
  407.3 0.4 convolution_subtract_fusion
  407.7 0.4 fusion.102
  408.1 3.1 fusion.2
  411.2 0.0 all-reduce.9.cloned.1.call-update
  411.2 94.5 %all-reduce.9.cloned.1.call-done = bf16[1792,256]{1,0:T(8,128)(2,1)} async-done(((bf16[1792,256]{1,0:T(8,128)(2,1)}), bf16[1792,256]{1,0:T(8,128)(2,1)}) %all-reduce.9.cloned.1.call-update) | async-done | bytes 917520 | tf_op jit(solution)/shard_map/psum | solution.py:12
  505.7 0.0 copy-start.1
  505.7 7.8 %subtract_convert_fusion = bf16[1792,1792]{1,0:T(8,128)(2,1)} fusion(bf16[1792,1792]{1,0:T(8,128)(2,1)} %fusion.7, bf16[1792,256]{1,0:T(8,128)(2,1)} %all-reduce.9.cloned.1.call-done, bf16[256,1792]{1,0:T(8,128)(2,1)S(1)} %copy-done.3, pred[1792]{0:T(1024)(128)(4,1)S(1)} %fusion.66), kind=kOutput, calls=%fused_computation.4 | convolution fusion | flops 1654259712 | bytes 14681856 | tf_op jit(solution)/shard_map/dot_general | solution.py:90
  513.5 0.0 copy-done.1
  513.5 3.3 fusion.5
  516.8 13.0 %reshape.600 = bf16[7,256,7,256]{3,2,1,0:T(8,128)(2,1)} reshape(bf16[1792,1792]{1,0:T(8,128)(2,1)} %fusion.5) | data formatting | bytes 12845056 | tf_op jit(solution)/shard_map/reshape | solution.py:96
  529.8 7.6 %copy.9 = bf16[7,256,7,256]{3,1,2,0:T(8,128)(2,1)} copy(bf16[7,256,7,256]{3,2,1,0:T(8,128)(2,1)} %reshape.600) | data formatting | bytes 12845056 | tf_op jit(solution)/shard_map/reshape | solution.py:96
  (14 shorter events, 0.2 us)
Async XLA Ops:
  6.5 139.4 %all-reduce.13.cloned.1.call-start = ((), (), s32[]{:S(2)}) async-start(), calls=%async_computation.3 | async-start | bytes 3670016 | tf_op jit(solution)/shard_map/psum | solution.py:12
  6.5 6.8 %copy-start.4 = (s32[2,256]{1,0:T(2,128)S(1)}, s32[2,256]{1,0:T(2,128)}, u32[]{:S(2)}) copy-start(s32[2,256]{1,0:T(2,128)} %param.11) | copy-start | bytes 6148
  13.4 5.6 %slice-start = ((bf16[7,256,7,256]{3,1,2,0:T(8,128)(2,1)}), bf16[1,256,7,256]{3,1,2,0:T(8,128)(2,1)S(1)}, s32[]{:S(2)}) async-start(bf16[7,256,7,256]{3,1,2,0:T(8,128)(2,1)} %param.10), calls=%async_computation.4 | async-start | bytes 1835008 | tf_op jit(solution)/shard_map/slice | solution.py:61
  28.1 229.6 %all-reduce.7.cloned.1.call-start = ((), (), s32[]{:S(2)}) async-start(), calls=%async_computation | async-start | bytes 1835008 | tf_op jit(solution)/shard_map/psum | solution.py:12
  145.9 9.5 %copy-start.2 = (bf16[256,1792]{1,0:T(8,128)(2,1)S(1)}, bf16[256,1792]{1,0:T(8,128)(2,1)}, u32[]{:S(2)}) copy-start(bf16[256,1792]{1,0:T(8,128)(2,1)} %get-tuple-element.56) | copy-start | bytes 2752516
  163.2 230.5 %all-reduce.11.cloned.1.call-start = ((), (), s32[]{:S(2)}) async-start(), calls=%async_computation.2 | async-start | bytes 3670016 | tf_op jit(solution)/shard_map/psum | solution.py:12
  257.7 7.8 %copy-start = (bf16[1792,256]{1,0:T(8,128)(2,1)S(1)}, bf16[1792,256]{1,0:T(8,128)(2,1)}, u32[]{:S(2)}) copy-start(bf16[1792,256]{1,0:T(8,128)(2,1)} %all-reduce.7.cloned.1.call-done) | copy-start | bytes 2752516
  277.2 228.5 %all-reduce.9.cloned.1.call-start = ((), (), s32[]{:S(2)}) async-start(), calls=%async_computation.1 | async-start | bytes 1835008 | tf_op jit(solution)/shard_map/psum | solution.py:12
  393.7 9.7 %copy-start.3 = (bf16[256,1792]{1,0:T(8,128)(2,1)S(1)}, bf16[256,1792]{1,0:T(8,128)(2,1)}, u32[]{:S(2)}) copy-start(bf16[256,1792]{1,0:T(8,128)(2,1)} %get-tuple-element.54) | copy-start | bytes 2752516
  505.7 7.8 %copy-start.1 = (bf16[1792,256]{1,0:T(8,128)(2,1)S(1)}, bf16[1792,256]{1,0:T(8,128)(2,1)}, u32[]{:S(2)}) copy-start(bf16[1792,256]{1,0:T(8,128)(2,1)} %all-reduce.9.cloned.1.call-done) | copy-start | bytes 2752516
Sparse Core Ops, SparseCore 0:
  28.2 117.6 all-reduce.12
  163.3 94.3 all-reduce.6
  277.4 116.2 all-reduce.10
  411.3 94.3 all-reduce.8
where the time goes:
time: 555 us; the launch traced here: 544 us
  waiting for transfers between devices  422 us (76%)
  local copies, waits for them, and re-layouts  65.8 us (12%)
  matrix products  26.3 us (5%)
  other arithmetic  15.8 us (3%)
  between operations  13.6 us (2%)
    psum x4, waiting for transfers between devices, broadcast(): return lax.psum(jnp.where(mine, shard, jnp.zeros_like(shard)), axis)  422 us
    reshape x2, local copies, waits for them, and re-layouts, body(): return current.reshape(row_cycles, block_size, col_cycles, block_size)  20.6 us
    scatter x2, local copies, waits for them, and re-layouts, body(): current = current.at[target].set(old_top, mode='drop')  19.2 us
    dot_general x2, matrix products, body(): jnp.dot(lower_panel, upper_rows, preferred_element_type=jnp.float32)  15.6 us
    unnamed x13, local copies, waits for them, and re-layouts  13 us
    gather x2, local copies, waits for them, and re-layouts, body(): current[jnp.clip(local_at, 0, local_rows - 1)]  11.6 us
  transfers between devices with their start and end apart: 4, of which 4 were waited for; matrix products, arithmetic and copies ran while one was open for 0% of the time, Pallas kernels for 0%

commit v1 on v0

v1 whole, which is shorter than its diff:
```python
import functools

import jax
import jax.numpy as jnp
from jax import lax
from jax.experimental import pallas as pl
from jax.experimental.pallas import tpu as pltpu
from jax.sharding import PartitionSpec as P

NEWTON = 3
BF = jnp.bfloat16
F32 = jnp.float32
MESH = pl.DeviceIdType.MESH
VM = pltpu.VMEM


def dot(a, b):
    return jnp.dot(a, b, preferred_element_type=F32)


def dot_full(a, b):
    return jnp.dot(a, b, precision=lax.Precision.HIGHEST, preferred_element_type=F32)


def split3(x):
    hi = x.astype(BF)
    rest = x - hi.astype(F32)
    mid = rest.astype(BF)
    low = (rest - mid.astype(F32)).astype(BF)
    return hi, mid, low


def dot_bf_f32(a, parts):
    hi, mid, low = parts
    return dot(a, low) + dot(a, mid) + dot(a, hi)


def newton_inverse(diag):
    n = diag.shape[0]
    row = lax.broadcasted_iota(jnp.int32, (n, n), 0)
    col = lax.broadcasted_iota(jnp.int32, (n, n), 1)
    eye = jnp.where(row == col, 1.0, 0.0).astype(F32)
    approx = eye / 3.0
    for _ in range(NEWTON):
        product = dot_full(diag, approx)
        approx = dot_full(approx, 2.0 * eye - product)
    return approx


def interchange(pivots, nb):
    first, second = pivots[0], pivots[1]
    lane = jnp.arange(nb, dtype=jnp.int32)
    same = second[:, None] == first[None, :]
    source_two = jnp.where(
        jnp.any(same, axis=1), jnp.sum(jnp.where(same, lane[None, :], 0), axis=1), second
    )
    source = jnp.concatenate([first, source_two])
    back = (lane + nb)[:, None] == first[None, :]
    after = jnp.where(
        jnp.any(back, axis=1), jnp.sum(jnp.where(back, lane[None, :], 0), axis=1), lane + nb
    )
    after = jnp.concatenate([first, after])
    moved = (after - nb)[:, None] == lane[None, :]
    lifted = after[:, None] == second[None, :]
    target = jnp.where(
        jnp.any(moved, axis=1),
        jnp.sum(jnp.where(moved, second[None, :], 0), axis=1),
        jnp.where(
            jnp.any(lifted, axis=1),
            jnp.sum(jnp.where(lifted, lane[None, :] + nb, 0), axis=1),
            after,
        ),
    )
    return source, target


def pick_kernel(nr, where_ref, m_ref, first_ref, rest_ref, hot):
    c = pl.program_id(0)
    cycles, _, nb, _ = m_ref.shape
    rows = cycles * nb
    r = lax.axis_index("row")

    @pl.when(c == 0)
    def _():
        at = lax.broadcasted_iota(jnp.int32, (2 * nb, rows), 1)
        hot[...] = jnp.where(at == where_ref[...], 1.0, 0.0).astype(BF)

    block = m_ref[...].reshape(rows, nb)
    picked = dot(hot[...], block).astype(BF)
    top = block[:nb]
    zero = jnp.zeros_like(top)
    own = [jnp.where(r == s, top, zero) for s in range(2)]

    def put(ref):
        ref[0, : 2 * nb] = picked
        ref[0, 2 * nb : 3 * nb] = own[0]
        ref[0, 3 * nb :] = own[1]

    @pl.when(c == 0)
    def _():
        put(first_ref)

    @pl.when(c > 0)
    def _():
        put(rest_ref)


def pick(matrix, where, nr):
    ra, ca, nb, _ = matrix.shape
    return pl.pallas_call(
        functools.partial(pick_kernel, nr),
        grid=(ca,),
        in_specs=[
            pl.BlockSpec((2 * nb, 1), lambda c: (0, 0)),
            pl.BlockSpec((ra, 1, nb, nb), lambda c: (0, c, 0, 0)),
        ],
        out_specs=[
            pl.BlockSpec((1, 4 * nb, nb), lambda c: (0, 0, 0)),
            pl.BlockSpec((1, 4 * nb, nb), lambda c: (jnp.maximum(c - 1, 0), 0, 0)),
        ],
        out_shape=[
            jax.ShapeDtypeStruct((1, 4 * nb, nb), BF),
            jax.ShapeDtypeStruct((ca - 1, 4 * nb, nb), BF),
        ],
        scratch_shapes=[VM((2 * nb, ra * nb), BF)],
        name="pick_rows",
    )(where, matrix)


def limits(nz):
    far = nz // 2
    return {(0, 0): far, (0, 1): far - 1, (1, 0): far - 1, (1, 1): far}


class RingSum:
    @staticmethod
    def scratch(nc, nz, q, nb):
        far = nz // 2
        dma = pltpu.SemaphoreType.DMA
        return [
            VM((nz, 2, nc, q, nb), BF),
            VM((2, 2, far, nc, q, nb), BF),
            VM((2, 2, far, nc, q, nb), BF),
            dma((2, nz, 2)),
            dma((2, 2, 2, far)),
            dma((2, 2, 2, far)),
            dma((2, nz, 2)),
        ]

    def __init__(self, nz, c_ref, out_ref, scratch):
        self.nz, self.c, self.out = nz, c_ref, out_ref
        (self.pbuf, self.sbuf, self.rbuf, self.psem, self.rsem, self.gsem, self.qsem) = scratch
        r = lax.axis_index("row")
        self.z, self.k = r // 2, r % 2
        self.partner = self.z * 2 + (1 - self.k)
        self.next = [
            ((self.z + nz - 1) % nz) * 2 + self.k,
            ((self.z + 1) % nz) * 2 + self.k,
        ]

    def peers(self):
        return [{"row": self.partner}, {"row": self.next[0]}, {"row": self.next[1]}]

    def at(self, offset):
        return (self.z + offset) % self.nz

    def copy(self, src, dst, send, recv, target):
        return pltpu.make_async_remote_copy(
            src_ref=src, dst_ref=dst, send_sem=send, recv_sem=recv,
            device_id={"row": target}, device_id_type=MESH,
        )

    def pair(self, slot, sub):
        t = self.at(slot)
        return self.copy(
            self.c.at[:, 1 - self.k, t, sub], self.pbuf.at[slot, sub],
            self.psem.at[0, slot, sub], self.psem.at[1, slot, sub], self.partner,
        )

    def reduce(self, way, sub, d):
        i = d - 1
        return self.copy(
            self.sbuf.at[way, sub, i], self.rbuf.at[way, sub, i],
            self.rsem.at[0, way, sub, i], self.rsem.at[1, way, sub, i], self.next[way],
        )

    def slot(self, way, d):
        return d % self.nz if way == 0 else (self.nz - d) % self.nz

    def spread(self, way, sub, d):
        t = self.at(self.slot(way, d - 1))
        i = d - 1
        piece = self.out.at[:, self.k, t, sub]
        return self.copy(
            piece, piece, self.gsem.at[0, way, sub, i], self.gsem.at[1, way, sub, i], self.next[way]
        )

    def arrived(self, way, sub, d):
        t = self.at(self.slot(way, d))
        i = d - 1
        piece = self.out.at[:, self.k, t, sub]
        self.copy(
            piece, piece, self.gsem.at[0, way, sub, i], self.gsem.at[1, way, sub, i], self.next[way]
        ).wait_recv()

    def share(self, slot, sub, core):
        piece = self.out.at[:, core, self.at(slot), sub]
        return self.copy(
            piece, piece, self.qsem.at[0, slot, sub], self.qsem.at[1, slot, sub], self.partner
        )

    def steps(self):
        nz, far, limit = self.nz, self.nz // 2, limits(self.nz)
        order = []
        for d in range(far, 0, -1):
            for slot in (self.slot(1, d), self.slot(0, d)):
                if slot not in order:
                    order.append(slot)
        order.append(0)
        for slot in order:
            for sub in range(2):
                self.pair(slot, sub).start()
        yield
        for d in range(far, 0, -1):
            for way, sub in limit:
                if d > limit[way, sub]:
                    continue
                slot = self.slot(1 - way, d)
                if not (d == far or (way == 1 and d == far)):
                    pass
                self.pair_once(slot, sub)
                value = self.c[:, self.k, self.at(slot), sub] + self.pbuf[slot, sub]
                if d < limit[way, sub]:
                    self.reduce(way, sub, d + 1).wait_recv()
                    value = value + self.rbuf[way, sub, d]
                self.sbuf[way, sub, d - 1] = value
                self.reduce(way, sub, d).start()
            yield
        for sub in range(2):
            self.pair_once(0, sub)
            value = self.c[:, self.k, self.z, sub] + self.pbuf[0, sub]
            for way in range(2):
                if limit[way, sub] >= 1:
                    self.reduce(way, sub, 1).wait_recv()
                    value = value + self.rbuf[way, sub, 0]
            self.out[:, self.k, self.z, sub] = value
            for way in range(2):
                if limit[way, sub] >= 1:
                    self.spread(way, sub, 1).start()
            self.share(0, sub, self.k).start()
        yield
        for d in range(1, far + 1):
            for way, sub in limit:
                if d > limit[way, sub]:
                    continue
                self.arrived(way, sub, d)
                if d < limit[way, sub]:
                    self.spread(way, sub, d + 1).start()
                self.share(self.slot(way, d), sub, self.k).start()
            yield
        for slot in range(nz):
            for sub in range(2):
                self.share(slot, sub, 1 - self.k).wait_recv()
        for slot in range(nz):
            for sub in range(2):
                self.pair(slot, sub).wait_send()
                self.share(slot, sub, self.k).wait_send()
        for (way, sub), top in limit.items():
            for d in range(1, top + 1):
                self.reduce(way, sub, d).wait_send()
                self.spread(way, sub, d).wait_send()

    seen = None

    def pair_once(self, slot, sub):
        if self.seen is None:
            self.seen = set()
        if (slot, sub) not in self.seen:
            self.seen.add((slot, sub))
            self.pair(slot, sub).wait_recv()


class PanelRelay:
    @staticmethod
    def scratch(parts):
        dma = pltpu.SemaphoreType.DMA
        return [dma((3, 2, 2, parts)), dma((2,))]

    def __init__(self, nx, ny, parts, src_ref, out_ref, scratch):
        self.nx, self.ny, self.parts = nx, ny, parts
        self.src, self.out = src_ref, out_ref
        self.sem, self.own_sem = scratch
        c = lax.axis_index("col")
        self.c, self.x, self.y = c, c // ny, c % ny
        self.height = src_ref.shape[0] // (2 * parts)

    def neighbours(self, way):
        nx, ny, x, y = self.nx, self.ny, self.x, self.y
        if way:
            return (x + 1) % nx * ny + y, x * ny + (y + 1) % ny
        return (x + nx - 1) % nx * ny + y, x * ny + (y + ny - 1) % ny

    def peers(self):
        return [{"col": n} for way in range(2) for n in self.neighbours(way)]

    def place(self, root, way):
        x0, y0 = root // self.ny, root % self.ny
        if way:
            return (self.x + self.nx - x0) % self.nx, (self.y + self.ny - y0) % self.ny
        return (x0 + self.nx - self.x) % self.nx, (y0 + self.ny - self.y) % self.ny

    def copy(self, root, way, part, axis):
        start = (way * self.parts + part) * self.height
        piece = self.out.at[root, pl.ds(start, self.height)]
        return pltpu.make_async_remote_copy(
            src_ref=piece, dst_ref=piece,
            send_sem=self.sem.at[axis, root, way, part],
            recv_sem=self.sem.at[2, root, way, part],
            device_id={"col": self.neighbours(way)[axis]}, device_id_type=MESH,
        )

    def sends(self, root, way, part, act):
        h, v = self.place(root, way)

        @pl.when(jnp.logical_and(v == 0, h < self.nx - 1))
        def _():
            act(self.copy(root, way, part, 0))

        @pl.when(v < self.ny - 1)
        def _():
            act(self.copy(root, way, part, 1))

    def steps(self):
        for root in range(2):
            @pl.when(self.c == root)
            def _():
                own = pltpu.make_async_copy(self.src, self.out.at[root], self.own_sem.at[root])
                own.start()
                own.wait()
        yield
        for part in range(self.parts):
            for root in range(2):
                for way in range(2):
                    @pl.when(self.c != root)
                    def _():
                        self.copy(root, way, part, 0).wait_recv()

                    self.sends(root, way, part, lambda copy: copy.start())
            yield
        for part in range(self.parts):
            for root in range(2):
                for way in range(2):
                    self.sends(root, way, part, lambda copy: copy.wait_send())


def greet(peers):
    barrier = pltpu.get_barrier_semaphore()
    for peer in peers:
        pl.semaphore_signal(barrier, inc=1, device_id=peer, device_id_type=MESH)
    pl.semaphore_wait(barrier, len(peers))


def run_all(plans):
    plans = list(plans)
    while plans:
        plans = [plan for plan in plans if next(plan, plan) is not plan]


def ring_kernel(nz, c_ref, out_ref, *scratch):
    ring = RingSum(nz, c_ref, out_ref, scratch)
    greet(ring.peers())
    run_all([ring.steps()])


def params(ident):
    return pltpu.CompilerParams(
        collective_id=ident, has_side_effects=True, vmem_limit_bytes=48 << 20
    )


def ring_sum(parts, nz, ident):
    nc, rows, nb = parts.shape
    q = rows // (4 * nz)
    shape = (nc, 2, nz, 2, q, nb)
    out = pl.pallas_call(
        functools.partial(ring_kernel, nz),
        out_shape=jax.ShapeDtypeStruct(shape, BF),
        in_specs=[pl.BlockSpec(memory_space=VM)],
        out_specs=pl.BlockSpec(memory_space=VM),
        scratch_shapes=RingSum.scratch(nc, nz, q, nb),
        compiler_params=params(ident),
        name="ring_sum",
    )(parts.reshape(shape))
    return out.reshape(nc, rows, nb)


def both_kernel(nz, nx, ny, parts, c_ref, src_ref, out_ref, panel_ref, *scratch):
    ring = RingSum(nz, c_ref, out_ref, scratch[:7])
    relay = PanelRelay(nx, ny, parts, src_ref, panel_ref, scratch[7:])
    greet(ring.peers() + relay.peers())
    run_all([relay.steps(), ring.steps()])


def ring_and_relay(rest, src, nz, nx, ny, parts, ident):
    nc, rows, nb = rest.shape
    q = rows // (4 * nz)
    shape = (nc, 2, nz, 2, q, nb)
    out, panel = pl.pallas_call(
        functools.partial(both_kernel, nz, nx, ny, parts),
        out_shape=[
            jax.ShapeDtypeStruct(shape, BF),
            jax.ShapeDtypeStruct((2,) + src.shape, BF),
        ],
        in_specs=[pl.BlockSpec(memory_space=VM)] * 2,
        out_specs=[pl.BlockSpec(memory_space=VM)] * 2,
        scratch_shapes=RingSum.scratch(nc, nz, q, nb) + PanelRelay.scratch(parts),
        compiler_params=params(ident),
        name="ring_and_relay",
    )(rest.reshape(shape), src)
    return out.reshape(nc, rows, nb), panel


def hot_rows(at_ref, a, nb):
    row = lax.broadcasted_iota(jnp.int32, (nb, 2 * nb), 0) + a * nb
    hot = jnp.where(row == at_ref[...], 1.0, 0.0)
    return hot.astype(BF), jnp.sum(hot, axis=1, keepdims=True) > 0.0


def panel_kernel(at_ref, m_ref, rows_ref, out_ref):
    cycles, _, nb, _ = m_ref.shape
    r = lax.axis_index("row")
    old = rows_ref[0, 2 * nb :]
    for a in range(cycles):
        hot, hit = hot_rows(at_ref, a, nb)
        value = jnp.where(hit, dot(hot, old).astype(BF), m_ref[a, 0])
        if a == 0:
            value = jnp.where(r == 0, rows_ref[0, :nb], value)
            value = jnp.where(r == 1, rows_ref[0, nb : 2 * nb], value)
        out_ref[a * nb : (a + 1) * nb] = value
    out_ref[cycles * nb :] = rows_ref[0, : 2 * nb]


def panel_rows(matrix, at, rows):
    ra, ca, nb, _ = matrix.shape
    return pl.pallas_call(
        panel_kernel,
        grid=(1,),
        in_specs=[
            pl.BlockSpec((1, 2 * nb), lambda i: (0, 0)),
            pl.BlockSpec((ra, 1, nb, nb), lambda i: (0, 0, 0, 0)),
            pl.BlockSpec((1, 4 * nb, nb), lambda i: (0, 0, 0)),
        ],
        out_specs=pl.BlockSpec(((ra + 2) * nb, nb), lambda i: (0, 0)),
        out_shape=jax.ShapeDtypeStruct(((ra + 2) * nb, nb), BF),
        name="panel_rows",
    )(at, matrix, rows)


def update_kernel(
    nr, at_ref, m_ref, first_ref, rest_ref, panel_ref, top_ref, out_ref, upper, inv, corner
):
    a = pl.program_id(0)
    _, nc, nb, _ = m_ref.shape
    r = lax.axis_index("row")
    col = lax.axis_index("col")

    def rows_of(c):
        return first_ref.at[0] if c == 0 else rest_ref.at[c - 1]

    @pl.when(a == 0)
    def _():
        inverse = split3(newton_inverse(top_ref[0, :nb].astype(F32)))
        for i in range(3):
            inv[0, i] = inverse[i]
        lower = dot_bf_f32(top_ref[0, nb:], inverse).astype(BF)
        corner[...] = top_ref[1, :nb]
        diag = (top_ref[1, nb:].astype(F32) - dot(lower, top_ref[1, :nb])).astype(BF)
        inverse = split3(newton_inverse(diag.astype(F32)))
        for i in range(3):
            inv[1, i] = inverse[i]
        for c in range(nc):
            one = rows_of(c)[:nb]
            if c == 0:
                one = jnp.where(col == 0, jnp.zeros_like(one), one)
            two = (rows_of(c)[nb : 2 * nb].astype(F32) - dot(lower, one)).astype(BF)
            if c == 0:
                two = jnp.where(col <= 1, jnp.zeros_like(two), two)
            upper[0, c] = one
            upper[1, c] = two

    zero = jnp.zeros((nb, nb), BF)
    block = a * nr + r
    lower0 = dot_bf_f32(panel_ref[0], [inv[0, i] for i in range(3)]).astype(BF)
    lower0 = jnp.where(block >= 1, lower0, zero)
    second = (panel_ref[1].astype(F32) - dot(lower0, corner[...])).astype(BF)
    lower1 = dot_bf_f32(second, [inv[1, i] for i in range(3)]).astype(BF)
    lower1 = jnp.where(block >= 2, lower1, zero)
    hot, hit = hot_rows(at_ref, a, nb)
    for c in range(nc):
        value = jnp.where(hit, dot(hot, rows_of(c)[2 * nb :]).astype(BF), m_ref[0, c])
        value = jnp.where(block == 0, rows_of(c)[:nb], value)
        value = jnp.where(block == 1, rows_of(c)[nb : 2 * nb], value)
        value = (value.astype(F32) - dot(lower0, upper[0, c])).astype(BF)
        value = (value.astype(F32) - dot(lower1, upper[1, c])).astype(BF)
        if c == 0:
            value = jnp.where(jnp.logical_and(col == 0, block >= 1), lower0, value)
            value = jnp.where(jnp.logical_and(col == 1, block >= 2), lower1, value)
        out_ref[0, c] = value


def update(matrix, at, first, rest, panel, nr):
    ra, ca, nb, _ = matrix.shape
    return pl.pallas_call(
        functools.partial(update_kernel, nr),
        grid=(ra,),
        in_specs=[
            pl.BlockSpec((1, 2 * nb), lambda a: (0, 0)),
            pl.BlockSpec((1, ca, nb, nb), lambda a: (a, 0, 0, 0)),
            pl.BlockSpec(first.shape, lambda a: (0, 0, 0)),
            pl.BlockSpec(rest.shape, lambda a: (0, 0, 0)),
            pl.BlockSpec((2, nb, nb), lambda a: (0, a, 0)),
            pl.BlockSpec((2, 2 * nb, nb), lambda a: (0, 0, 0)),
        ],
        out_specs=pl.BlockSpec((1, ca, nb, nb), lambda a: (a, 0, 0, 0)),
        out_shape=jax.ShapeDtypeStruct(matrix.shape, BF),
        scratch_shapes=[
            VM((2, ca, nb, nb), BF),
            VM((2, 3, nb, nb), BF),
            VM((nb, nb), BF),
        ],
        compiler_params=pltpu.CompilerParams(vmem_limit_bytes=48 << 20),
        name="update",
    )(at, matrix, first, rest, panel, panel[:, ra * nb :])


def body(nr, nx, ny, parts, matrix, pivots):
    r = lax.axis_index("row")
    matrix = matrix.transpose(0, 2, 1, 3)
    nb = matrix.shape[2]
    source, target = interchange(pivots, nb)

    def local(rows, valid):
        index = rows // (nb * nr) * nb + rows % nb
        return jnp.where(jnp.logical_and(valid, rows // nb % nr == r), index, -1)

    where = local(source, True)[:, None]
    at = local(target, target >= 2 * nb)[None, :]
    first, rest = pick(matrix, where, nr)
    first = ring_sum(first, nr // 2, 1)
    src = panel_rows(matrix, at, first)
    rest, panel = ring_and_relay(rest, src, nr // 2, nx, ny, parts, 2)
    out = update(matrix, at, first, rest, panel, nr)
    return out.transpose(0, 2, 1, 3)


def solution(mesh):
    nr, ncol = mesh.shape["row"], mesh.shape["col"]
    ny = int(ncol**0.5)
    return jax.shard_map(
        functools.partial(body, nr, ncol // ny, ny, 8),
        mesh=mesh,
        in_specs=(P(None, "row", None, "col"), P()),
        out_specs=P(None, "row", None, "col"),
        check_vma=False,
    )
```

time: 555 us -> 420 us (0.76); the launches traced: 544 us -> 420 us
  waiting for transfers between devices: 422 us -> 0 us
  Pallas kernels: 0 us -> 413 us
  local copies, waits for them, and re-layouts: 65.8 us -> 4.04 us
  matrix products: 26.3 us -> 0 us
  between operations: 13.6 us -> 0.09 us
  other arithmetic: 15.8 us -> 3.06 us
    psum x4 -> x0, waiting for transfers between devices: 422 us -> none  [broadcast(): return lax.psum(jnp.where(mine, shard, jnp.zeros_like(shard)), axis)]
    pallas_call x0 -> x5, Pallas kernels: none -> 413 us  [the longest x1 344 us: ring_and_relay(): pl.pallas_call(functools.partial(both_kernel, nz, nx, ny, parts), out_sha...]
    dot_general x16 -> x0, matrix products: 26.3 us -> none  [the longest x2 15.6 us: body(): jnp.dot(lower_panel, upper_rows, preferred_element_type=jnp.float32)]
    reshape x2 -> x0, local copies, waits for them, and re-layouts: 20.6 us -> none  [body(): return current.reshape(row_cycles, block_size, col_cycles, block_size)]
    scatter x2 -> x0, local copies, waits for them, and re-layouts: 19.2 us -> none  [body(): current = current.at[target].set(old_top, mode='drop')]
    gather x2 -> x0, local copies, waits for them, and re-layouts: 11.6 us -> none  [body(): current[jnp.clip(local_at, 0, local_rows - 1)]]
    scatter x4 -> x0, other arithmetic: 11.2 us -> none  [the longest x2 6.62 us: body(): current.at[:, panel_cycle * block_size:(panel_cycle + 1) * block_size]]
    unnamed x13 -> x10, local copies, waits for them, and re-layouts: 13 us -> 3.1 us
  transfers between devices with their start and end apart: 4 -> 0, of which waited for: 4 -> 0; matrix products, arithmetic and copies ran while one was open for 0% -> 0% of each run, Pallas kernels for 0% -> 0%
where the time goes in v1:
time: 420 us
  Pallas kernels  413 us (98%)
    pallas_call x1, Pallas kernels, ring_and_relay(): pl.pallas_call(functools.partial(both_kernel, nz, nx, ny, parts), out_sha...  344 us
    pallas_call x1, Pallas kernels, ring_sum(): pl.pallas_call(functools.partial(ring_kernel, nz), out_shape=jax.ShapeDty...  34 us
    pallas_call x1, Pallas kernels, update(): pl.pallas_call(functools.partial(update_kernel, nr), grid=(ra,), in_specs...  22 us
    pallas_call x1, Pallas kernels, pick(): pl.pallas_call(functools.partial(pick_kernel, nr), grid=(ca,), in_specs=[...  9.41 us

profile of v1, /device:TPU:3, one launch (start us, length us, event | category | flops | bytes accessed | tf_op | source)
XLA Modules:
  0.0 420.1 jit_solution(10857427710900120585)
XLA Ops:
  0.0 0.8 slice_bitcast_fusion
  0.8 0.3 compare_reduce_fusion.1
  1.0 0.3 fusion.3
  1.3 0.4 compare_reduce_fusion
  1.7 0.4 fusion
  2.1 0.6 and_select_fusion.2.at_ref
  2.7 0.1 copy.9
  2.8 1.2 fusion.9.where_ref
  4.0 9.4 %pick_rows.1 = (bf16[1,1024,256]{2,1,0:T(8,128)(2,1)}, bf16[6,1024,256]{2,1,0:T(8,128)(2,1)}) custom-call(s32[512,1]{1,0:T(8,128)} %fusion.9.where_ref, bf16[7,7,256,256]{3,2,1,0:T(8,128)(2,1)} %bitcast.17), custom_call_target="tpu_custom_call" | custom-call | tf_op jit(solution)/shard_map/pick_rows/pallas_call | solution.py:110
  13.4 0.0 copy-start.3
  13.4 1.0 copy-done.3
  14.5 34.0 %ring_sum.1 = bf16[1,2,8,2,32,256]{5,4,3,2,1,0:T(8,128)(2,1)S(1)} custom-call(bf16[1,2,8,2,32,256]{5,4,3,2,1,0:T(8,128)(2,1)S(1)} %bitcast.16), custom_call_target="tpu_custom_call" | custom-call | tf_op jit(solution)/shard_map/ring_sum/pallas_call | solution.py:385
  48.5 0.0 copy-start
  48.5 0.8 copy-done
  49.3 3.1 panel_rows.1.src_ref
  52.4 0.0 copy-start.2
  52.4 1.3 copy-done.2
  53.7 0.0 copy-start.1
  53.7 0.0 copy-start.4
  53.7 344.3 %ring_and_relay.1 = (bf16[6,2,8,2,32,256]{5,4,3,2,1,0:T(8,128)(2,1)}, bf16[2,2304,256]{2,1,0:T(8,128)(2,1)S(1)}) custom-call(bf16[6,2,8,2,32,256]{5,4,3,2,1,0:T(8,128)(2,1)} %bitcast.21, bf16[2304,256]{1,0:T(8,128)(2,1)S(1)} %copy-done.2), custom_call_target="tpu_custom_call" | custom-call | tf_op jit(solution)/shard_map/ring_and_relay/pallas_call | solution.py:408
  398.1 0.0 copy-done.1
  398.1 0.0 copy-done.4
  398.1 22.0 %update.1 = bf16[7,7,256,256]{3,2,1,0:T(8,128)(2,1)} custom-call(s32[1,512]{1,0:T(1,128)S(1)} %copy-done.4, bf16[7,7,256,256]{3,2,1,0:T(8,128)(2,1)} %bitcast.19, bf16[1,1024,256]{2,1,0:T(8,128)(2,1)S(1)} %bitcast.15, bf16[6,1024,256]{2,1,0:T(8,128)(2,1)} %bitcast.20, bf16[2,2304,256]{2,1,0:T(8,128)(2,1)S(1)} %get-tuple-element.12.panel_ref, ...), custom_call_target="tpu_custom_call" | custom-call | tf_op jit(solution)/shard_map/update/pallas_call | solution.py:513
  (6 shorter events, 0.1 us)
Async XLA Ops:
  13.4 1.0 copy-start.3
  48.5 0.8 copy-start
  52.4 1.3 copy-start.2
  53.7 344.4 %copy-start.1 = (bf16[1,2,8,2,32,256]{5,4,3,2,1,0:T(8,128)(2,1)S(1)}, bf16[1,2,8,2,32,256]{5,4,3,2,1,0:T(8,128)(2,1)}, u32[]{:S(2)}) copy-start(bf16[1,2,8,2,32,256]{5,4,3,2,1,0:T(8,128)(2,1)} %copy-done) | copy-start | bytes 1572868
  53.7 344.4 %copy-start.4 = (s32[1,512]{1,0:T(1,128)S(1)}, s32[1,512]{1,0:T(1,128)}, u32[]{:S(2)}) copy-start(s32[1,512]{1,0:T(1,128)} %and_select_fusion.2.at_ref) | copy-start | bytes 6148

commit v2 on v1

--- a/solution.py
+++ b/solution.py
@@ -74,7 +74,7 @@
     return source, target
 
 
-def pick_kernel(nr, where_ref, m_ref, first_ref, rest_ref, hot):
+def pick_kernel(where_ref, m_ref, first_ref, rest_ref, src_ref, hot):
     c = pl.program_id(0)
     cycles, _, nb, _ = m_ref.shape
     rows = cycles * nb
@@ -99,16 +99,18 @@
     @pl.when(c == 0)
     def _():
         put(first_ref)
+        src_ref[0] = block[:, : nb // 2]
+        src_ref[1] = block[:, nb // 2 :]
 
     @pl.when(c > 0)
     def _():
         put(rest_ref)
 
 
-def pick(matrix, where, nr):
+def pick(matrix, where):
     ra, ca, nb, _ = matrix.shape
     return pl.pallas_call(
-        functools.partial(pick_kernel, nr),
+        pick_kernel,
         grid=(ca,),
         in_specs=[
             pl.BlockSpec((2 * nb, 1), lambda c: (0, 0)),
@@ -117,10 +119,12 @@
         out_specs=[
             pl.BlockSpec((1, 4 * nb, nb), lambda c: (0, 0, 0)),
             pl.BlockSpec((1, 4 * nb, nb), lambda c: (jnp.maximum(c - 1, 0), 0, 0)),
+            pl.BlockSpec((2, ra * nb, nb // 2), lambda c: (0, 0, 0)),
         ],
         out_shape=[
             jax.ShapeDtypeStruct((1, 4 * nb, nb), BF),
             jax.ShapeDtypeStruct((ca - 1, 4 * nb, nb), BF),
+            jax.ShapeDtypeStruct((2, ra * nb, nb // 2), BF),
         ],
         scratch_shapes=[VM((2 * nb, ra * nb), BF)],
         name="pick_rows",
@@ -226,8 +230,6 @@
                 if d > limit[way, sub]:
                     continue
                 slot = self.slot(1 - way, d)
-                if not (d == far or (way == 1 and d == far)):
-                    pass
                 self.pair_once(slot, sub)
                 value = self.c[:, self.k, self.at(slot), sub] + self.pbuf[slot, sub]
                 if d < limit[way, sub]:
@@ -280,77 +282,120 @@
             self.pair(slot, sub).wait_recv()
 
 
-class PanelRelay:
+class PlaneCast:
     @staticmethod
-    def scratch(parts):
+    def scratch(nx, ny):
         dma = pltpu.SemaphoreType.DMA
-        return [dma((3, 2, 2, parts)), dma((2,))]
-
-    def __init__(self, nx, ny, parts, src_ref, out_ref, scratch):
-        self.nx, self.ny, self.parts = nx, ny, parts
-        self.src, self.out = src_ref, out_ref
-        self.sem, self.own_sem = scratch
-        c = lax.axis_index("col")
-        self.c, self.x, self.y = c, c // ny, c % ny
-        self.height = src_ref.shape[0] // (2 * parts)
-
-    def neighbours(self, way):
-        nx, ny, x, y = self.nx, self.ny, self.x, self.y
-        if way:
-            return (x + 1) % nx * ny + y, x * ny + (y + 1) % ny
-        return (x + nx - 1) % nx * ny + y, x * ny + (y + ny - 1) % ny
+        far = max(nx, ny) // 2
+        return [dma((nx * ny,)), dma((2,)), dma((2, 2, 2, 2, far)), dma((2,))]
+
+    def __init__(self, nx, ny, src_ref, out_ref, scratch):
+        self.n, self.src, self.out = (nx, ny), src_ref, out_ref
+        self.far_sem, self.near_sem, self.ring_sem, self.share_sem = scratch
+        self.c = lax.axis_index("col")
+        self.pos = self.c // ny, self.c % ny
+
+    def step(self, axis, way):
+        x, y = self.pos
+        nx, ny = self.n
+        if axis == 0:
+            return (x + (1 if way else nx - 1)) % nx * ny + y
+        return x * ny + (y + (1 if way else ny - 1)) % ny
 
     def peers(self):
-        return [{"col": n} for way in range(2) for n in self.neighbours(way)]
-
-    def place(self, root, way):
-        x0, y0 = root // self.ny, root % self.ny
-        if way:
-            return (self.x + self.nx - x0) % self.nx, (self.y + self.ny - y0) % self.ny
-        return (x0 + self.nx - self.x) % self.nx, (y0 + self.ny - self.y) % self.ny
-
-    def copy(self, root, way, part, axis):
-        start = (way * self.parts + part) * self.height
-        piece = self.out.at[root, pl.ds(start, self.height)]
+        nx, ny = self.n
+        found = [{"col": self.step(axis, way)} for axis in range(2) for way in range(2)]
+        return found
+
+    def copy(self, src, dst, send, recv, target):
         return pltpu.make_async_remote_copy(
-            src_ref=piece, dst_ref=piece,
-            send_sem=self.sem.at[axis, root, way, part],
-            recv_sem=self.sem.at[2, root, way, part],
-            device_id={"col": self.neighbours(way)[axis]}, device_id_type=MESH,
-        )
-
-    def sends(self, root, way, part, act):
-        h, v = self.place(root, way)
-
-        @pl.when(jnp.logical_and(v == 0, h < self.nx - 1))
+            src_ref=src, dst_ref=dst, send_sem=send, recv_sem=recv,
+            device_id={"col": target}, device_id_type=MESH,
+        )
+
+    def far(self, i):
+        nx, ny = self.n
+        t = (self.c + i) % (nx * ny)
+        return self.copy(
+            self.src.at[:, t // ny, t % ny], self.out.at[self.c, :, t // ny, t % ny],
+            self.far_sem.at[i], self.near_sem.at[self.c], t,
+        )
+
+    def keep(self):
+        x, y = self.pos
+        self.out[self.c, :, x, y] = self.src[:, x, y]
+
+    def near(self, root):
+        piece = self.out.at[root, :, self.pos[0], self.pos[1]]
+        return self.copy(piece, piece, self.far_sem.at[0], self.near_sem.at[root], root)
+
+    def piece(self, half, phase, q, roots):
+        axis = half if phase == 0 else 1 - half
+        if phase == 1:
+            if axis == 0:
+                return self.out.at[roots, half, q]
+            return self.out.at[roots, half, :, q]
+        if axis == 0:
+            return self.out.at[roots, half, q, self.pos[1]]
+        return self.out.at[roots, half, self.pos[0], q]
+
+    def ring(self, half, phase, way, d, origin):
+        axis = half if phase == 0 else 1 - half
+        n = self.n[axis]
+        roots = slice(None) if d < n // 2 else way
+        q = (self.pos[axis] + (origin if way == 0 else n - origin)) % n
+        piece = self.piece(half, phase, q, roots)
+        sem = self.ring_sem
+        return self.copy(
+            piece, piece, sem.at[0, half, phase, way, d - 1], sem.at[1, half, phase, way, d - 1],
+            self.step(axis, way),
+        )
+
+    def kinds(self, phase):
+        for half in range(2):
+            for way in range(2):
+                yield half, way, self.n[half if phase == 0 else 1 - half] // 2
+
+    def steps(self):
+        total = self.n[0] * self.n[1]
+
+        @pl.when(self.c < 2)
         def _():
-            act(self.copy(root, way, part, 0))
-
-        @pl.when(v < self.ny - 1)
+            for i in range(total - 1, 0, -1):
+                self.far(i).start()
+
+        yield
+        for root in range(2):
+            @pl.when(self.c != root)
+            def _():
+                self.near(root).wait_recv()
+
+        for phase in range(2):
+            top = 0
+            for half, way, far in self.kinds(phase):
+                self.ring(half, phase, way, 1, 0).start()
+                top = max(top, far)
+            for d in range(1, top + 1):
+                yield
+                for half, way, far in self.kinds(phase):
+                    if d <= far:
+                        self.ring(half, phase, way, d, d).wait_recv()
+                    if d < far:
+                        if d + 1 < far:
+                            self.ring(half, phase, way, d + 1, d).start()
+                        else:
+                            self.ring(half, phase, way, d + 1, d).start()
+        yield
+
+        @pl.when(self.c < 2)
         def _():
-            act(self.copy(root, way, part, 1))
-
-    def steps(self):
-        for root in range(2):
-            @pl.when(self.c == root)
-            def _():
-                own = pltpu.make_async_copy(self.src, self.out.at[root], self.own_sem.at[root])
-                own.start()
-                own.wait()
-        yield
-        for part in range(self.parts):
-            for root in range(2):
-                for way in range(2):
-                    @pl.when(self.c != root)
-                    def _():
-                        self.copy(root, way, part, 0).wait_recv()
-
-                    self.sends(root, way, part, lambda copy: copy.start())
-            yield
-        for part in range(self.parts):
-            for root in range(2):
-                for way in range(2):
-                    self.sends(root, way, part, lambda copy: copy.wait_send())
+            for i in range(total - 1, 0, -1):
+                self.far(i).wait_send()
+
+        for phase in range(2):
+            for half, way, far in self.kinds(phase):
+                for d in range(1, far + 1):
+                    self.ring(half, phase, way, d, d - 1).wait_send()
 
 
 def greet(peers):
@@ -360,64 +405,112 @@
     pl.semaphore_wait(barrier, len(peers))
 
 
-def run_all(plans):
-    plans = list(plans)
-    while plans:
-        plans = [plan for plan in plans if next(plan, plan) is not plan]
-
-
-def ring_kernel(nz, c_ref, out_ref, *scratch):
-    ring = RingSum(nz, c_ref, out_ref, scratch)
-    greet(ring.peers())
-    run_all([ring.steps()])
-
-
 def params(ident):
     return pltpu.CompilerParams(
         collective_id=ident, has_side_effects=True, vmem_limit_bytes=48 << 20
     )
 
 
-def ring_sum(parts, nz, ident):
-    nc, rows, nb = parts.shape
-    q = rows // (4 * nz)
-    shape = (nc, 2, nz, 2, q, nb)
-    out = pl.pallas_call(
-        functools.partial(ring_kernel, nz),
-        out_shape=jax.ShapeDtypeStruct(shape, BF),
-        in_specs=[pl.BlockSpec(memory_space=VM)],
-        out_specs=pl.BlockSpec(memory_space=VM),
-        scratch_shapes=RingSum.scratch(nc, nz, q, nb),
-        compiler_params=params(ident),
-        name="ring_sum",
-    )(parts.reshape(shape))
-    return out.reshape(nc, rows, nb)
-
-
-def both_kernel(nz, nx, ny, parts, c_ref, src_ref, out_ref, panel_ref, *scratch):
-    ring = RingSum(nz, c_ref, out_ref, scratch[:7])
-    relay = PanelRelay(nx, ny, parts, src_ref, panel_ref, scratch[7:])
-    greet(ring.peers() + relay.peers())
-    run_all([relay.steps(), ring.steps()])
-
-
-def ring_and_relay(rest, src, nz, nx, ny, parts, ident):
+def exchange_kernel(
+    nz, nx, ny, first_ref, rest_ref, src_ref, first_out, rest_out, panel_out, top_out, *scratch
+):
+    half = rest_ref.shape[0] // 2
+    slow = rest_ref.shape[0] - half
+    rings = [
+        RingSum(nz, first_ref, first_out, scratch[:7]),
+        RingSum(nz, rest_ref.at[:slow], rest_out.at[:slow], scratch[7:14]),
+    ]
+    rest = scratch[14:]
+    if half:
+        rings.append(RingSum(nz, rest_ref.at[slow:], rest_out.at[slow:], scratch[14:21]))
+        rest = scratch[21:]
+    core = rings[0].k
+    panel = PlaneCast(nx, ny, src_ref, panel_out, rest[:4])
+    stage = rest[8]
+    top = PlaneCast(nx, ny, stage, top_out.at[core], rest[4:8])
+    col = panel.c
+    total = nx * ny
+    lanes = src_ref.shape[-1]
+
+    @pl.when(col < 2)
+    def _():
+        panel.keep()
+
+    corners = [{"col": (col + i) % total} for i in range(1, total)]
+    greet(rings[0].peers() + corners)
+
+    def top_steps():
+        @pl.when(col < 2)
+        def _():
+            for sub in range(2):
+                part = first_out[0, core, :, :, :, sub * lanes : (sub + 1) * lanes]
+                stage[sub] = part.reshape(stage.shape[1:])
+            top.keep()
+
+        yield from top.steps()
+        mine, other = top_out.at[core], top_out.at[1 - core]
+
+        def share(ref):
+            return rings[0].copy(
+                ref, ref, top.share_sem.at[0], top.share_sem.at[1], rings[0].partner
+            )
+
+        share(mine).start()
+        share(other).wait_recv()
+        share(mine).wait_send()
+
+    plans = {"X": panel.steps(), "T": top_steps()}
+    for name, ring in zip("FAB", rings):
+        plans[name] = ring.steps()
+    for name in ORDER:
+        if name in plans:
+            next(plans[name], None)
+    for name in "FTXAB":
+        if name in plans:
+            for _ in plans[name]:
+                pass
+
+
+ORDER = "XFABFFABFFXABFFXABFFXABFFXTABTXABTXABTABTAB"
+
+
+def exchange(first, rest, src, nz, nx, ny, ident):
     nc, rows, nb = rest.shape
     q = rows // (4 * nz)
-    shape = (nc, 2, nz, 2, q, nb)
-    out, panel = pl.pallas_call(
-        functools.partial(both_kernel, nz, nx, ny, parts),
+    half = nc // 2
+    total = nx * ny
+
+    def grid(n):
+        return (n, 2, nz, 2, q, nb)
+
+    wide = src.shape[1]
+    plane = (2, nx, ny, wide // total, nb // 2)
+    corner = (2, 2, 2, nx, ny, 2 * nb // total, nb // 2)
+    scratch = RingSum.scratch(1, nz, q, nb) + RingSum.scratch(nc - half, nz, q, nb)
+    if half:
+        scratch += RingSum.scratch(half, nz, q, nb)
+    scratch += PlaneCast.scratch(nx, ny) + PlaneCast.scratch(nx, ny)
+    scratch.append(VM(corner[2:], BF))
+    first, rest, panel, top = pl.pallas_call(
+        functools.partial(exchange_kernel, nz, nx, ny),
         out_shape=[
-            jax.ShapeDtypeStruct(shape, BF),
-            jax.ShapeDtypeStruct((2,) + src.shape, BF),
+            jax.ShapeDtypeStruct(grid(1), BF),
+            jax.ShapeDtypeStruct(grid(nc), BF),
+            jax.ShapeDtypeStruct((2,) + plane, BF),
+            jax.ShapeDtypeStruct(corner, BF),
         ],
-        in_specs=[pl.BlockSpec(memory_space=VM)] * 2,
-        out_specs=[pl.BlockSpec(memory_space=VM)] * 2,
-        scratch_shapes=RingSum.scratch(nc, nz, q, nb) + PanelRelay.scratch(parts),
+        in_specs=[pl.BlockSpec(memory_space=VM)] * 3,
+        out_specs=[pl.BlockSpec(memory_space=VM)] * 4,
+        scratch_shapes=scratch,
         compiler_params=params(ident),
-        name="ring_and_relay",
-    )(rest.reshape(shape), src)
-    return out.reshape(nc, rows, nb), panel
+        name="exchange",
+    )(first.reshape(grid(1)), rest.reshape(grid(nc)), src.reshape(plane))
+    return (
+        first.reshape(1, rows, nb),
+        rest.reshape(nc, rows, nb),
+        panel.reshape(2, 2, wide, nb // 2),
+        top.reshape(2, 2, 2, 2 * nb, nb // 2),
+    )
 
 
 def hot_rows(at_ref, a, nb):
@@ -426,38 +519,8 @@
     return hot.astype(BF), jnp.sum(hot, axis=1, keepdims=True) > 0.0
 
 
-def panel_kernel(at_ref, m_ref, rows_ref, out_ref):
-    cycles, _, nb, _ = m_ref.shape
-    r = lax.axis_index("row")
-    old = rows_ref[0, 2 * nb :]
-    for a in range(cycles):
-        hot, hit = hot_rows(at_ref, a, nb)
-        value = jnp.where(hit, dot(hot, old).astype(BF), m_ref[a, 0])
-        if a == 0:
-            value = jnp.where(r == 0, rows_ref[0, :nb], value)
-            value = jnp.where(r == 1, rows_ref[0, nb : 2 * nb], value)
-        out_ref[a * nb : (a + 1) * nb] = value
-    out_ref[cycles * nb :] = rows_ref[0, : 2 * nb]
-
-
-def panel_rows(matrix, at, rows):
-    ra, ca, nb, _ = matrix.shape
-    return pl.pallas_call(
-        panel_kernel,
-        grid=(1,),
-        in_specs=[
-            pl.BlockSpec((1, 2 * nb), lambda i: (0, 0)),
-            pl.BlockSpec((ra, 1, nb, nb), lambda i: (0, 0, 0, 0)),
-            pl.BlockSpec((1, 4 * nb, nb), lambda i: (0, 0, 0)),
-        ],
-        out_specs=pl.BlockSpec(((ra + 2) * nb, nb), lambda i: (0, 0)),
-        out_shape=jax.ShapeDtypeStruct(((ra + 2) * nb, nb), BF),
-        name="panel_rows",
-    )(at, matrix, rows)
-
-
 def update_kernel(
-    nr, at_ref, m_ref, first_ref, rest_ref, panel_ref, top_ref, out_ref, upper, inv, corner
+    nr, at_ref, m_ref, first_ref, rest_ref, panel_ref, top_ref, out_ref, upper, inv, heads
 ):
     a = pl.program_id(0)
     _, nc, nb, _ = m_ref.shape
@@ -467,14 +530,19 @@
     def rows_of(c):
         return first_ref.at[0] if c == 0 else rest_ref.at[c - 1]
 
+    def whole(ref, *at):
+        return jnp.concatenate([ref[at + (0,)], ref[at + (1,)]], axis=-1)
+
     @pl.when(a == 0)
     def _():
-        inverse = split3(newton_inverse(top_ref[0, :nb].astype(F32)))
+        for i in range(2):
+            for root in range(2):
+                heads[i, root] = whole(top_ref, i, root)
+        inverse = split3(newton_inverse(heads[0, 0, :nb].astype(F32)))
         for i in range(3):
             inv[0, i] = inverse[i]
-        lower = dot_bf_f32(top_ref[0, nb:], inverse).astype(BF)
-        corner[...] = top_ref[1, :nb]
-        diag = (top_ref[1, nb:].astype(F32) - dot(lower, top_ref[1, :nb])).astype(BF)
+        lower = dot_bf_f32(heads[0, 0, nb:], inverse).astype(BF)
+        diag = (heads[0, 1, nb:].astype(F32) - dot(lower, heads[0, 1, :nb])).astype(BF)
         inverse = split3(newton_inverse(diag.astype(F32)))
         for i in range(3):
             inv[1, i] = inverse[i]
@@ -490,16 +558,21 @@
 
     zero = jnp.zeros((nb, nb), BF)
     block = a * nr + r
-    lower0 = dot_bf_f32(panel_ref[0], [inv[0, i] for i in range(3)]).astype(BF)
+    hot, hit = hot_rows(at_ref, a, nb)
+
+    def swapped(old, top, mine):
+        value = jnp.where(hit, dot(hot, old).astype(BF), mine)
+        value = jnp.where(block == 0, top[:nb], value)
+        return jnp.where(block == 1, top[nb:], value)
+
+    panels = [swapped(heads[1, p], heads[0, p], whole(panel_ref, p)) for p in range(2)]
+    lower0 = dot_bf_f32(panels[0], [inv[0, i] for i in range(3)]).astype(BF)
     lower0 = jnp.where(block >= 1, lower0, zero)
-    second = (panel_ref[1].astype(F32) - dot(lower0, corner[...])).astype(BF)
+    second = (panels[1].astype(F32) - dot(lower0, heads[0, 1, :nb])).astype(BF)
     lower1 = dot_bf_f32(second, [inv[1, i] for i in range(3)]).astype(BF)
     lower1 = jnp.where(block >= 2, lower1, zero)
-    hot, hit = hot_rows(at_ref, a, nb)
     for c in range(nc):
-        value = jnp.where(hit, dot(hot, rows_of(c)[2 * nb :]).astype(BF), m_ref[0, c])
-        value = jnp.where(block == 0, rows_of(c)[:nb], value)
-        value = jnp.where(block == 1, rows_of(c)[nb : 2 * nb], value)
+        value = swapped(rows_of(c)[2 * nb :], rows_of(c)[: 2 * nb], m_ref[0, c])
         value = (value.astype(F32) - dot(lower0, upper[0, c])).astype(BF)
         value = (value.astype(F32) - dot(lower1, upper[1, c])).astype(BF)
         if c == 0:
@@ -508,7 +581,7 @@
         out_ref[0, c] = value
 
 
-def update(matrix, at, first, rest, panel, nr):
+def update(matrix, at, first, rest, panel, top, nr):
     ra, ca, nb, _ = matrix.shape
     return pl.pallas_call(
         functools.partial(update_kernel, nr),
@@ -518,22 +591,22 @@
             pl.BlockSpec((1, ca, nb, nb), lambda a: (a, 0, 0, 0)),
             pl.BlockSpec(first.shape, lambda a: (0, 0, 0)),
             pl.BlockSpec(rest.shape, lambda a: (0, 0, 0)),
-            pl.BlockSpec((2, nb, nb), lambda a: (0, a, 0)),
-            pl.BlockSpec((2, 2 * nb, nb), lambda a: (0, 0, 0)),
+            pl.BlockSpec((2, 2, nb, nb // 2), lambda a: (0, 0, a, 0)),
+            pl.BlockSpec(top.shape, lambda a: (0, 0, 0, 0, 0)),
         ],
         out_specs=pl.BlockSpec((1, ca, nb, nb), lambda a: (a, 0, 0, 0)),
         out_shape=jax.ShapeDtypeStruct(matrix.shape, BF),
         scratch_shapes=[
             VM((2, ca, nb, nb), BF),
             VM((2, 3, nb, nb), BF),
-            VM((nb, nb), BF),
+            VM((2, 2, 2 * nb, nb), BF),
         ],
         compiler_params=pltpu.CompilerParams(vmem_limit_bytes=48 << 20),
         name="update",
-    )(at, matrix, first, rest, panel, panel[:, ra * nb :])
-
-
-def body(nr, nx, ny, parts, matrix, pivots):
+    )(at, matrix, first, rest, panel, top)
+
+
+def body(nr, nx, ny, matrix, pivots):
     r = lax.axis_index("row")
     matrix = matrix.transpose(0, 2, 1, 3)
     nb = matrix.shape[2]
@@ -545,11 +618,9 @@
 
     where = local(source, True)[:, None]
     at = local(target, target >= 2 * nb)[None, :]
-    first, rest = pick(matrix, where, nr)
-    first = ring_sum(first, nr // 2, 1)
-    src = panel_rows(matrix, at, first)
-    rest, panel = ring_and_relay(rest, src, nr // 2, nx, ny, parts, 2)
-    out = update(matrix, at, first, rest, panel, nr)
+    first, rest, src = pick(matrix, where)
+    first, rest, panel, top = exchange(first, rest, src, nr // 2, nx, ny, 1)
+    out = update(matrix, at, first, rest, panel, top, nr)
     return out.transpose(0, 2, 1, 3)
 
 
@@ -557,7 +628,7 @@
     nr, ncol = mesh.shape["row"], mesh.shape["col"]
     ny = int(ncol**0.5)
     return jax.shard_map(
-        functools.partial(body, nr, ncol // ny, ny, 8),
+        functools.partial(body, nr, ncol // ny, ny),
         mesh=mesh,
         in_specs=(P(None, "row", None, "col"), P()),
         out_specs=P(None, "row", None, "col"),

time: 420 us -> 112 us (0.27)
  Pallas kernels: 413 us -> 106 us
    pallas_call x4 -> x2, Pallas kernels: 391 us -> 82.3 us  [the longest x1 72.4 us: exchange(): pl.pallas_call(functools.partial(exchange_kernel, nz, nx, ny), out_shape=...]
where the time goes in v2:
time: 112 us; the launch traced here: 111 us
  Pallas kernels  106 us (95%)
  local copies, waits for them, and re-layouts  3.13 us (3%)
  other arithmetic  2.47 us (2%)
    pallas_call x1, Pallas kernels, exchange(): pl.pallas_call(functools.partial(exchange_kernel, nz, nx, ny), out_shape=...  72.4 us
    pallas_call x1, Pallas kernels, update(): pl.pallas_call(functools.partial(update_kernel, nr), grid=(ra,), in_specs...  23.4 us
    pallas_call x1, Pallas kernels, pick(): pl.pallas_call(pick_kernel, grid=(ca,), in_specs=[pl.BlockSpec((2 * nb, 1...  9.91 us

profile of v2, /device:TPU:3, one launch (start us, length us, event | category | flops | bytes accessed | tf_op | source)
XLA Modules:
  0.0 111.4 jit_solution(17014093004557022296)
XLA Ops:
  0.0 0.8 slice_bitcast_fusion
  0.8 0.3 compare_reduce_fusion.1
  1.0 0.3 fusion.3
  1.3 0.4 compare_reduce_fusion
  1.7 0.4 fusion
  2.1 0.1 copy.9
  2.3 1.1 %fusion.9.where_ref = s32[512,1]{1,0:T(8,128)} fusion(s32[512,1]{1,0:T(8,128)S(1)} %copy.9, s32[]{:T(128)S(6)} %axis_index.15), kind=kLoop, calls=%fused_computation.28 | loop fusion | flops 22528 | bytes 4100 | tf_op jit(solution)/shard_map/jit(_where)/select_n | solution.py:617
  3.4 9.9 %pick_rows.1 = (bf16[1,1024,256]{2,1,0:T(8,128)(2,1)}, bf16[6,1024,256]{2,1,0:T(8,128)(2,1)}, bf16[2,1792,128]{2,1,0:T(8,128)(2,1)}) custom-call(s32[512,1]{1,0:T(8,128)} %fusion.9.where_ref, bf16[7,7,256,256]{3,2,1,0:T(8,128)(2,1)} %bitcast.22), custom_call_target="tpu_custom_call" | custom-call | tf_op jit(solution)/shard_map/pick_rows/pallas_call | solution.py:112
  13.3 0.0 copy-start
  13.3 1.2 %copy-done = bf16[2,1792,128]{2,1,0:T(8,128)(2,1)S(1)} copy-done((bf16[2,1792,128]{2,1,0:T(8,128)(2,1)S(1)}, bf16[2,1792,128]{2,1,0:T(8,128)(2,1)}, u32[]{:S(2)}) %copy-start) | copy-done | bytes 917528
  14.5 0.0 copy-start.1
  14.5 1.0 copy-done.1
  15.6 72.4 %exchange.1 = (bf16[1,2,8,2,32,256]{5,4,3,2,1,0:T(8,128)(2,1)S(1)}, bf16[6,2,8,2,32,256]{5,4,3,2,1,0:T(8,128)(2,1)}, bf16[2,2,4,4,112,128]{5,4,3,2,1,0:T(8,128)(2,1)S(1)}, bf16[2,2,2,4,4,32,128]{6,5,4,3,2,1,0:T(8,128)(2,1)S(1)}) custom-call(bf16[1,2,8,2,32,256]{5,4,3,2,1,0:T(8,128)(2,1)S(1)} %bitcast.20, bf16[6,2,8,2,32,256]{5,4,3,2,1,0:T(8,128)(2,1)} %bitcast.25, ...), custom_call_target="tpu_custom_call" | custom-call | tf_op jit(solution)/shard_map/exchange/pallas_call | solution.py:494
  88.0 23.4 %update.1 = bf16[7,7,256,256]{3,2,1,0:T(8,128)(2,1)} custom-call(s32[1,512]{1,0:T(1,128)S(1)} %and_select_fusion.2.at_ref, bf16[7,7,256,256]{3,2,1,0:T(8,128)(2,1)} %bitcast.23, bf16[1,1024,256]{2,1,0:T(8,128)(2,1)S(1)} %bitcast.21, bf16[6,1024,256]{2,1,0:T(8,128)(2,1)} %bitcast.24, bf16[2,2,1792,128]{3,2,1,0:T(8,128)(2,1)S(1)} %bitcast.17, ...), custom_call_target="tpu_custom_call" | custom-call | tf_op jit(solution)/shard_map/update/pallas_call | solution.py:586
  (6 shorter events, 0.1 us)
Async XLA Ops:
  13.3 1.2 %copy-start = (bf16[2,1792,128]{2,1,0:T(8,128)(2,1)S(1)}, bf16[2,1792,128]{2,1,0:T(8,128)(2,1)}, u32[]{:S(2)}) copy-start(bf16[2,1792,128]{2,1,0:T(8,128)(2,1)} %get-tuple-element.14) | copy-start | bytes 2752516
  14.5 1.0 copy-start.1
